TPU v7x, 32 devices: a whole 2x2x4 slice. The times are simulated.
32 devices in a mesh: wide: 8 (over y, x, core), blk: 4 (over z).
Axes of the slice: x: 2, y: 2, z: 4, core: 2. Of those that a mesh axis runs over, the one named last changes fastest.
Arguments:
- visual_features: bfloat16 [32768, 1152], P(('wide', 'blk')), may hold values from -0.1875 to 0.1875
- sentence_features: bfloat16 [1024, 1152], P(('wide', 'blk')), may hold values from -0.1875 to 0.1875
- true_partner_ids: int32 [32768], P(('wide', 'blk')), may hold values from 0 to 1023
- inverse_warmth: float32 [], replicated, may hold values from 90 to 110
- additive_adjust: float32 [], replicated, may hold values from -12 to -9
Outputs:
- grad_images: float32 [32768, 1152], P(('wide', 'blk'))
- grad_texts: float32 [1024, 1152], P(('wide', 'blk'))
Inputs may be any that keep to these rules, and one draw needn't show every extreme that they name: Image i is paired with text true_partner_ids[i]; a text may be paired with several images or none.
All inputs are finite; a program needn't handle non-finite values.
Results may differ from a plain program's by a relative error of at most 0.007.
Values may be sent and summed in bfloat16 or wider, within the bound.
No kernel may reach another device: no remote copies, remote signals or barrier semaphores. Data moves between devices by JAX's collectives and lax.ppermute only.
A program may use at most 64 MiB of HBM per device.

v0:
```python
import jax
import jax.numpy as jnp
from jax import lax
from jax.sharding import PartitionSpec as P


def remaining_factors(
    visual_features, tile_length, true_partner_ids, leading_offset, inverse_warmth, additive_adjust
):
    cosine_grid = lax.dot_general(
        visual_features, tile_length, (((1,), (1,)), ((), ())), preferred_element_type=jnp.float32
    )
    sigmoid_levels = inverse_warmth * cosine_grid + additive_adjust
    columns = leading_offset + lax.iota(jnp.int32, tile_length.shape[0])
    plus_minus_ones = jnp.where(true_partner_ids[:, None] == columns[None, :], 1.0, -1.0).astype(
        jnp.float32
    )
    return (
        -inverse_warmth * plus_minus_ones * jax.nn.sigmoid(-plus_minus_ones * sigmoid_levels)
    ).astype(jnp.bfloat16)


def both_grads(visual_features, tile_length, loss_grid_scaled):
    incoming_grad_part = jnp.dot(loss_grid_scaled, tile_length, preferred_element_type=jnp.float32)
    returned_grad_part = lax.dot_general(
        loss_grid_scaled,
        visual_features,
        (((0,), (0,)), ((), ())),
        preferred_element_type=jnp.float32,
    )
    return (incoming_grad_part, returned_grad_part)


def shards(visual_features, sentence_features, true_partner_ids, inverse_warmth, additive_adjust):
    width = visual_features.shape[1]
    everything = lax.all_gather(sentence_features, ("wide", "blk"), axis=0, tiled=True)
    total = everything.shape[0]
    block = min(total, 1024)
    count = total // block
    blocks = everything.reshape(count, block, width)

    def scan_step(grad_img, running_dot_sums):
        piece, leading_offset = running_dot_sums
        loss_grid_scaled = remaining_factors(
            visual_features,
            piece,
            true_partner_ids,
            leading_offset,
            inverse_warmth,
            additive_adjust,
        )
        incoming_grad_part, returned_grad_part = both_grads(
            visual_features, piece, loss_grid_scaled
        )
        return (grad_img + incoming_grad_part, returned_grad_part)

    firsts = lax.iota(jnp.int32, count) * block
    grad_images, grad_blocks = lax.scan(
        scan_step, jnp.zeros(visual_features.shape, jnp.float32), (blocks, firsts)
    )
    grad_texts = lax.psum_scatter(
        grad_blocks.reshape(total, width), ("wide", "blk"), scatter_dimension=0, tiled=True
    )
    return (grad_images, grad_texts)


def solution(mesh):
    return jax.shard_map(
        shards,
        mesh=mesh,
        in_specs=(P(("wide", "blk"), None), P(("wide", "blk"), None), P(("wide", "blk")), P(), P()),
        out_specs=(P(("wide", "blk"), None), P(("wide", "blk"), None)),
        check_vma=False,
    )
```

profile of v0, /device:TPU:0, one launch (start us, length us, event | category | flops | bytes accessed | tf_op | source)
XLA Modules:
  0.0 195.8 jit_solution(3945152771545359974)
XLA Ops:
  7.2 0.0 copy-start
  7.2 0.0 all-gather.2.cloned.1.call-start
  7.2 0.7 all-gather.2.cloned.1.call-update
  7.9 0.0 reduce-scatter.2.cloned.1.call-start
  9.3 61.3 %all-gather.2.cloned.1.call-done = bf16[1024,1152]{1,0:T(8,128)(2,1)} async-done(((bf16[32,1152]{1,0:T(8,128)(2,1)}), bf16[1024,1152]{1,0:T(8,128)(2,1)}) %all-gather.2.cloned.1.call-update) | async-done | bytes 2359312 | tf_op jit(solution)/shard_map/all_gather | solution.py:36
  70.6 0.0 copy-done
  70.6 5.9 %fusion.1 = bf16[1024,1024]{1,0:T(8,128)(2,1)S(1)} fusion(bf16[1024,1152]{1,0:T(8,128)(2,1)S(1)} %copy-done, bf16[1024,1152]{1,0:T(8,128)(2,1)} %all-gather.2.cloned.1.call-done, f32[]{:T(128)S(6)} %copy.8, f32[]{:T(128)S(6)} %copy.7, s32[1024]{0:T(1024)} %param.7, f32[]{:T(128)S(6)} %neg.12), kind=kOutput, calls=%fused_computation.3 | convolution fusion | flops 2428502016 | bytes 6819852 | tf_op jit(solution)/shard_map/while/body/eval_jaxpr/dot_general | solution.py:10
  76.5 0.0 copy-start.1
  76.5 1.4 copy-done.1
  77.9 4.6 %fusion.8 = f32[1024,1152]{1,0:T(8,128)} fusion(bf16[1024,1024]{1,0:T(8,128)(2,1)S(1)} %fusion.1, bf16[1024,1152]{1,0:T(8,128)(2,1)S(1)} %copy-done), kind=kOutput, calls=%fused_computation.11 | convolution fusion | flops 2415919104 | bytes 9175040 | tf_op jit(solution)/shard_map/while/body/eval_jaxpr/dot_general | solution.py:25
  82.5 0.0 reduce-scatter.2.cloned.1.call-update
  82.5 7.4 %fusion.7 = f32[1024,1152]{1,0:T(8,128)} fusion(bf16[1024,1024]{1,0:T(8,128)(2,1)} %copy-done.1, bf16[1024,1152]{1,0:T(8,128)(2,1)} %all-gather.2.cloned.1.call-done), kind=kOutput, calls=%fused_computation.10 | convolution fusion | flops 2415919104 | bytes 9175040 | tf_op jit(solution)/shard_map/while/body/eval_jaxpr/dot_general | solution.py:24
  89.9 99.1 %reduce-scatter.2.cloned.1.call-done = f32[32,1152]{1,0:T(8,128)} async-done(((f32[1024,1152]{1,0:T(8,128)}), f32[32,1152]{1,0:T(8,128)}) %reduce-scatter.2.cloned.1.call-update) | async-done | bytes 147472 | tf_op jit(solution)/shard_map/reduce_scatter | solution.py:61
Async XLA Ops:
  7.2 63.4 %copy-start = (bf16[1024,1152]{1,0:T(8,128)(2,1)S(1)}, bf16[1024,1152]{1,0:T(8,128)(2,1)}, u32[]{:S(2)}) copy-start(bf16[1024,1152]{1,0:T(8,128)(2,1)} %param.5) | copy-start | bytes 7077892
  7.2 63.4 %all-gather.2.cloned.1.call-start = ((), (), s32[]{:S(2)}) async-start(), calls=%async_computation.1 | async-start | bytes 2433024 | tf_op jit(solution)/shard_map/all_gather | solution.py:36
  7.9 181.0 %reduce-scatter.2.cloned.1.call-start = ((), (), s32[]{:S(2)}) async-start(), calls=%async_computation.2 | async-start | bytes 4866048 | tf_op jit(solution)/shard_map/reduce_scatter | solution.py:61
  76.5 1.4 copy-start.1
Sparse Core Ops, SparseCore 0:
  10.8 59.7 all-gather.1
  82.6 106.2 reduce-scatter.1
where the time goes:
time: 196 us
  waiting for transfers between devices  161 us (82%)
  matrix products  17.9 us (9%)
  between operations  15.4 us (8%)
    reduce_scatter x1, waiting for transfers between devices, shards(): lax.psum_scatter(grad_blocks.reshape(total, width), ('wide', 'blk'), scat...  99.1 us
    all_gather x1, waiting for transfers between devices, shards(): lax.all_gather(sentence_features, ('wide', 'blk'), axis=0, tiled=True)  61.3 us
    dot_general x1, matrix products, both_grads(): jnp.dot(loss_grid_scaled, tile_length, preferred_element_type=jnp.float32)  7.36 us
    dot_general x1, matrix products, remaining_factors(): lax.dot_general(visual_features, tile_length, (((1,), (1,)), ((), ())), p...  5.92 us
    dot_general x1, matrix products, both_grads(): lax.dot_general(loss_grid_scaled, visual_features, (((0,), (0,)), ((), ()...  4.57 us
  transfers between devices with their start and end apart: 2, of which 2 were waited for; matrix products, arithmetic and copies ran while one was open for 4% of the time, Pallas kernels for 0%

commit v1 on v0

--- a/solution.py
+++ b/solution.py
@@ -33,7 +33,22 @@
 
 def shards(visual_features, sentence_features, true_partner_ids, inverse_warmth, additive_adjust):
     width = visual_features.shape[1]
-    everything = lax.all_gather(sentence_features, ("wide", "blk"), axis=0, tiled=True)
+    ways, here, step = (
+        lax.axis_size(("wide", "blk")),
+        lax.axis_index(("wide", "blk")),
+        sentence_features.shape[0],
+    )
+    line, have = (sentence_features, 1)
+    while have < ways:
+        line = jnp.concatenate(
+            [
+                line,
+                lax.ppermute(line, ("wide", "blk"), [(d, (d - have) % ways) for d in range(ways)]),
+            ],
+            axis=0,
+        )
+        have = 2 * have
+    everything = jnp.roll(line, here * step, axis=0)
     total = everything.shape[0]
     block = min(total, 1024)
     count = total // block

time: 196 us -> 215 us (1.097)
  local copies, waits for them, and re-layouts: 1.39 us -> 16.8 us
  starting transfers between devices: 0.08 us -> 9.9 us
  waiting for transfers between devices: 161 us -> 152 us
  other arithmetic: 0 us -> 2.85 us
    all_gather x1 -> x0, waiting for transfers between devices: 61.3 us -> none  [shards(): lax.all_gather(sentence_features, ('wide', 'blk'), axis=0, tiled=True)]
    ppermute x0 -> x5, waiting for transfers between devices: none -> 51.7 us  [shards(): lax.ppermute(line, ('wide', 'blk'), [(d, (d - have) % ways) for d in rang...]
    unnamed x4 -> x24, local copies, waits for them, and re-layouts: 1.39 us -> 14.5 us
    ppermute x0 -> x5, starting transfers between devices: none -> 9.86 us  [shards(): lax.ppermute(line, ('wide', 'blk'), [(d, (d - have) % ways) for d in rang...]
    concatenate x0 -> x3, other arithmetic: none -> 2.85 us  [shards(): jnp.concatenate([line, lax.ppermute(line, ('wide', 'blk'), [(d, (d - have...]
    concatenate x0 -> x2, local copies, waits for them, and re-layouts: none -> 2.28 us  [the longest x1 1.17 us: shards(): jnp.concatenate([line, lax.ppermute(line, ('wide', 'blk'), [(d, (d - have...]
  transfers between devices with their start and end apart: 2 -> 6, of which waited for: 2 -> 6; matrix products, arithmetic and copies ran while one was open for 4% -> 5% of each run, Pallas kernels for 0% -> 0%
where the time goes in v1:
time: 215 us
  waiting for transfers between devices  152 us (71%)
  matrix products  17.9 us (8%)
  local copies, waits for them, and re-layouts  16.8 us (8%)
  between operations  15.4 us (7%)
  starting transfers between devices  9.9 us (5%)
  other arithmetic  2.85 us (1%)
    reduce_scatter x1, waiting for transfers between devices, shards(): lax.psum_scatter(grad_blocks.reshape(total, width), ('wide', 'blk'), scat...  100 us
    ppermute x5, waiting for transfers between devices, shards(): lax.ppermute(line, ('wide', 'blk'), [(d, (d - have) % ways) for d in rang...  51.7 us
    unnamed x24, local copies, waits for them, and re-layouts  14.5 us
    ppermute x5, starting transfers between devices, shards(): lax.ppermute(line, ('wide', 'blk'), [(d, (d - have) % ways) for d in rang...  9.86 us
    dot_general x1, matrix products, both_grads(): jnp.dot(loss_grid_scaled, tile_length, preferred_element_type=jnp.float32)  7.42 us
    dot_general x1, matrix products, remaining_factors(): lax.dot_general(visual_features, tile_length, (((1,), (1,)), ((), ())), p...  5.95 us
    dot_general x1, matrix products, both_grads(): lax.dot_general(loss_grid_scaled, visual_features, (((0,), (0,)), ((), ()...  4.51 us
  transfers between devices with their start and end apart: 6, of which 6 were waited for; matrix products, arithmetic and copies ran while one was open for 5% of the time, Pallas kernels for 0%

profile of v1, /device:TPU:0, one launch (start us, length us, event | category | flops | bytes accessed | tf_op | source)
XLA Modules:
  0.0 214.7 jit_solution(7712883847037105522)
XLA Ops:
  7.2 6.5 %collective-permute-start = (bf16[32,1152]{1,0:T(8,128)(2,1)}, bf16[32,1152]{1,0:T(8,128)(2,1)S(1)}, u32[]{:S(2)}, u32[]{:S(2)}) collective-permute-start(bf16[32,1152]{1,0:T(8,128)(2,1)} %param.6), channel_id=1, source_target_pairs={{0,31},{1,0},{2,1},{3,2},{4,3},{5,4},{6,5},{7,6},{8,7},{9,8},{10,9... | collective-permute-start | bytes 221192 | tf_op jit(solution)/shard_map/ppermute | solution.py:46
  13.7 2.3 %collective-permute-done = bf16[32,1152]{1,0:T(8,128)(2,1)S(1)} collective-permute-done((bf16[32,1152]{1,0:T(8,128)(2,1)}, bf16[32,1152]{1,0:T(8,128)(2,1)S(1)}, u32[]{:S(2)}, u32[]{:S(2)}) %collective-permute-start) | collective-permute-done | bytes 73760 | tf_op jit(solution)/shard_map/ppermute | solution.py:46
  17.1 8.3 %collective-permute-done.1 = bf16[64,1152]{1,0:T(8,128)(2,1)S(1)} collective-permute-done((bf16[64,1152]{1,0:T(8,128)(2,1)S(1)}, bf16[64,1152]{1,0:T(8,128)(2,1)S(1)}, u32[]{:S(2)}, u32[]{:S(2)}) %collective-permute-start.1) | collective-permute-done | bytes 147488 | tf_op jit(solution)/shard_map/ppermute | solution.py:46
  25.4 1.0 pad_maximum_fusion.1
  26.4 1.7 collective-permute-start.2
  28.0 1.5 constant_dynamic-update-slice_fusion.4
  29.6 2.7 %collective-permute-done.2 = bf16[128,1152]{1,0:T(8,128)(2,1)S(1)} collective-permute-done((bf16[128,1152]{1,0:T(8,128)(2,1)S(1)}, bf16[128,1152]{1,0:T(8,128)(2,1)S(1)}, u32[]{:S(2)}, u32[]{:S(2)}) %collective-permute-start.2) | collective-permute-done | bytes 294944 | tf_op jit(solution)/shard_map/ppermute | solution.py:46
  32.3 1.0 pad_maximum_fusion
  33.3 1.2 collective-permute-start.3
  36.7 12.4 %collective-permute-done.3 = bf16[256,1152]{1,0:T(8,128)(2,1)S(1)} collective-permute-done((bf16[256,1152]{1,0:T(8,128)(2,1)S(1)}, bf16[256,1152]{1,0:T(8,128)(2,1)S(1)}, u32[]{:S(2)}, u32[]{:S(2)}) %collective-permute-start.3) | collective-permute-done | bytes 589856 | tf_op jit(solution)/shard_map/ppermute | solution.py:46
  49.0 1.2 constant_dynamic-update-slice_fusion
  52.0 26.0 %collective-permute-done.4 = bf16[512,1152]{1,0:T(8,128)(2,1)S(1)} collective-permute-done((bf16[512,1152]{1,0:T(8,128)(2,1)}, bf16[512,1152]{1,0:T(8,128)(2,1)S(1)}, u32[]{:S(2)}, u32[]{:S(2)}) %collective-permute-start.4) | collective-permute-done | bytes 1179680 | tf_op jit(solution)/shard_map/ppermute | solution.py:46
  78.0 1.1 constant_dynamic-update-slice_fusion.11
  79.1 1.5 constant_dynamic-update-slice_fusion.10
  80.6 1.5 constant_dynamic-update-slice_fusion.9
  82.1 1.6 constant_dynamic-update-slice_fusion.8
  83.7 1.7 constant_dynamic-update-slice_fusion.7
  85.4 1.9 constant_dynamic-update-slice_fusion.6
  87.3 1.1 constant_dynamic-update-slice_fusion.5
  88.5 5.9 %fusion.1 = bf16[1024,1024]{0,1:T(8,128)(2,1)S(1)} fusion(bf16[1024,1152]{1,0:T(8,128)(2,1)S(1)} %copy-done, f32[]{:T(128)S(6)} %copy.23, f32[]{:T(128)S(6)} %copy.22, s32[1024]{0:T(1024)S(1)} %copy-done.6, f32[]{:T(128)S(6)} %neg.12, bf16[2048,1152]{1,0:T(8,128)(2,1)} %constant_dynamic-update-slice_fusion.5, s32[]{:T(128)S(6)} %select_n.20), kind=kOutput, calls=%fused_computation.3 | convolution fusion | flops 2428502016 | bytes 6819856 | tf_op jit(solution)/shard_map/while/body/eval_jaxpr/dot_general | solution.py:10
  94.4 1.3 copy-done.4
  95.7 4.5 %fusion.12 = f32[1024,1152]{1,0:T(8,128)} fusion(bf16[1024,1024]{0,1:T(8,128)(2,1)S(1)} %fusion.1, bf16[1024,1152]{1,0:T(8,128)(2,1)S(1)} %copy-done), kind=kOutput, calls=%fused_computation.35 | convolution fusion | flops 2415919104 | bytes 9175040 | tf_op jit(solution)/shard_map/while/body/eval_jaxpr/dot_general | solution.py:25
  100.3 7.4 %fusion.7 = f32[1024,1152]{1,0:T(8,128)} fusion(bf16[1024,1024]{0,1:T(8,128)(2,1)} %copy-done.4, bf16[2048,1152]{1,0:T(8,128)(2,1)} %constant_dynamic-update-slice_fusion.5, s32[]{:T(128)S(6)} %select_n.20), kind=kOutput, calls=%fused_computation.10 | convolution fusion | flops 2415919104 | bytes 9175044 | tf_op jit(solution)/shard_map/while/body/eval_jaxpr/dot_general | solution.py:24
  107.7 100.2 %reduce-scatter.2.cloned.1.call-done = f32[32,1152]{1,0:T(8,128)} async-done(((f32[1024,1152]{1,0:T(8,128)}), f32[32,1152]{1,0:T(8,128)}) %reduce-scatter.2.cloned.1.call-update) | async-done | bytes 147472 | tf_op jit(solution)/shard_map/reduce_scatter | solution.py:76
  (21 shorter events, 3.9 us)
Async XLA Ops:
  7.2 81.3 %copy-start = (bf16[1024,1152]{1,0:T(8,128)(2,1)S(1)}, bf16[1024,1152]{1,0:T(8,128)(2,1)}, u32[]{:S(2)}) copy-start(bf16[1024,1152]{1,0:T(8,128)(2,1)} %param.5) | copy-start | bytes 7077892
  7.2 200.7 %reduce-scatter.2.cloned.1.call-start = ((), (), s32[]{:S(2)}) async-start(), calls=%async_computation.1 | async-start | bytes 4866048 | tf_op jit(solution)/shard_map/reduce_scatter | solution.py:76
  7.2 8.8 %collective-permute-start = (bf16[32,1152]{1,0:T(8,128)(2,1)}, bf16[32,1152]{1,0:T(8,128)(2,1)S(1)}, u32[]{:S(2)}, u32[]{:S(2)}) collective-permute-start(bf16[32,1152]{1,0:T(8,128)(2,1)} %param.6), channel_id=1, source_target_pairs={{0,31},{1,0},{2,1},{3,2},{4,3},{5,4},{6,5},{7,6},{8,7},{9,8},{10,9... | collective-permute-start | bytes 221192 | tf_op jit(solution)/shard_map/ppermute | solution.py:46
  16.0 34.7 %copy-start.5 = (bf16[32,1152]{1,0:T(8,128)(2,1)}, bf16[32,1152]{1,0:T(8,128)(2,1)S(1)}, u32[]{:S(2)}) copy-start(bf16[32,1152]{1,0:T(8,128)(2,1)S(1)} %collective-permute-done) | copy-start | bytes 221188
  16.9 8.5 %collective-permute-start.1 = (bf16[64,1152]{1,0:T(8,128)(2,1)S(1)}, bf16[64,1152]{1,0:T(8,128)(2,1)S(1)}, u32[]{:S(2)}, u32[]{:S(2)}) collective-permute-start(bf16[64,1152]{1,0:T(8,128)(2,1)S(1)} %pad_maximum_fusion.2), channel_id=1, source_target_pairs={{0,30},{1,31},{2,0},{3,1},{4,2},{5,3},{6,4},{7,5},{8,6},{9,7},{10,... | collective-permute-start | bytes 442376 | tf_op jit(solution)/shard_map/ppermute | solution.py:46
  25.4 25.3 %copy-start.3 = (bf16[64,1152]{1,0:T(8,128)(2,1)}, bf16[64,1152]{1,0:T(8,128)(2,1)S(1)}, u32[]{:S(2)}) copy-start(bf16[64,1152]{1,0:T(8,128)(2,1)S(1)} %collective-permute-done.1) | copy-start | bytes 442372
  26.4 5.9 %collective-permute-start.2 = (bf16[128,1152]{1,0:T(8,128)(2,1)S(1)}, bf16[128,1152]{1,0:T(8,128)(2,1)S(1)}, u32[]{:S(2)}, u32[]{:S(2)}) collective-permute-start(bf16[128,1152]{1,0:T(8,128)(2,1)S(1)} %pad_maximum_fusion.1), channel_id=1, source_target_pairs={{0,28},{1,29},{2,30},{3,31},{4,0},{5,1},{6,2},{7,3},{8,4},{9,5},{1... | collective-permute-start | bytes 884744 | tf_op jit(solution)/shard_map/ppermute | solution.py:46
  32.3 17.9 %copy-start.1 = (bf16[128,1152]{1,0:T(8,128)(2,1)}, bf16[128,1152]{1,0:T(8,128)(2,1)S(1)}, u32[]{:S(2)}) copy-start(bf16[128,1152]{1,0:T(8,128)(2,1)S(1)} %collective-permute-done.2) | copy-start | bytes 884740
  33.3 15.8 %collective-permute-start.3 = (bf16[256,1152]{1,0:T(8,128)(2,1)S(1)}, bf16[256,1152]{1,0:T(8,128)(2,1)S(1)}, u32[]{:S(2)}, u32[]{:S(2)}) collective-permute-start(bf16[256,1152]{1,0:T(8,128)(2,1)S(1)} %pad_maximum_fusion), channel_id=1, source_target_pairs={{0,24},{1,25},{2,26},{3,27},{4,28},{5,29},{6,30},{7,31},{8,0},{9,1... | collective-permute-start | bytes 1769480 | tf_op jit(solution)/shard_map/ppermute | solution.py:46
  49.0 1.2 copy-start.2
  49.0 39.4 %copy-start.6 = (s32[1024]{0:T(1024)S(1)}, s32[1024]{0:T(1024)}, u32[]{:S(2)}) copy-start(s32[1024]{0:T(1024)} %param.7) | copy-start | bytes 12292
  50.2 27.7 %collective-permute-start.4 = (bf16[512,1152]{1,0:T(8,128)(2,1)}, bf16[512,1152]{1,0:T(8,128)(2,1)S(1)}, u32[]{:S(2)}, u32[]{:S(2)}) collective-permute-start(bf16[512,1152]{1,0:T(8,128)(2,1)} %get-tuple-element.18), channel_id=1, source_target_pairs={{0,16},{1,17},{2,18},{3,19},{4,20},{5,21},{6,22},{7,23},{8,24},{9,... | collective-permute-start | bytes 3538952 | tf_op jit(solution)/shard_map/ppermute | solution.py:46
  94.4 1.3 copy-start.4
Sparse Core Ops, SparseCore 0:
  100.4 107.4 reduce-scatter.1
